TPU v7x, 512 devices: a whole 4x8x8 slice. The times are simulated.
512 devices in a mesh: grid: 32 (over y_lo, z, core), occ: 16 (over x, y_hi).
Axes of the slice: x: 4, y: 8 (y_hi: 4, y_lo: 2; y = y_hi * 2 + y_lo), z: 8, core: 2. Of those that a mesh axis runs over, the one named last changes fastest.
Arguments:
- orbital_values: bfloat16 [8192, 16000], P('grid', 'occ'), may hold values from -6 to 6
- occupied: bfloat16 [16000, 512], P('occ', 'grid'), may hold values from -0.046875 to 0.046875
- trial: bfloat16 [16000, 512], P('occ', 'grid'), may hold values from -0.046875 to 0.046875
- point_weights: float32 [8192], P('grid'), may hold values from 0.1 to 1
- batch_sizes: int32 [256], P('grid'), may hold values from 1 to 32, 4096 in all
- significant: int32 [256, 128], P('grid', 'occ'), may hold values 0 or 1
Outputs:
- exchange: float32 [16000, 512], P('occ', 'grid')
Inputs may be any that keep to these rules, and one draw needn't show every extreme that they name: `batch_sizes`: batch sizes sum to 4096 and the largest is exactly 32.
All inputs are finite; a program needn't handle non-finite values. No bound on the sum of `batch_sizes` or of `significant` on one device may be relied on, other than what follows from the above.
Results may differ from a plain program's by a relative error of at most 0.0027.
Values may be sent and summed in bfloat16 or wider, within the bound.
A program may use at most 64 MiB of HBM per device.

v0:
```python
import math
import jax
import jax.numpy as jnp
from jax import lax
from jax.sharding import PartitionSpec as P


def screen(values, sizes, significant):
    rows, cols = values.shape
    batches = sizes.shape[0]
    blocks = significant.shape[1]
    blocked = (
        values.reshape(batches, rows // batches, blocks, cols // blocks)
        * significant.astype(values.dtype)[:, None, :, None]
    )
    position = lax.broadcasted_iota(jnp.int32, (batches, rows // batches), 1)
    live = (position < sizes[:, None]).astype(jnp.float32).reshape(rows)
    return (blocked.reshape(rows, cols), live)


def per_device(orbital_values, occupied, trial, point_weights, batch_sizes, significant):
    screened, live = screen(orbital_values, batch_sizes, significant)
    rows = screened.shape[0]
    grid_count = lax.axis_size("grid")
    columns = occupied.shape[1]
    total = columns * grid_count
    joined = jnp.concatenate((occupied, trial), axis=1)
    panels_all = lax.all_gather(joined, "grid", axis=1, tiled=True)
    terms = jnp.dot(screened, panels_all, preferred_element_type=jnp.float32)
    stacked = (
        terms.reshape(rows, grid_count, 2, columns).transpose(0, 2, 1, 3).reshape(rows, 2, total)
    )
    weight = point_weights * live
    occ_scale = 1.0 / math.sqrt(total)
    shares = lax.psum_scatter(stacked, "occ", scatter_dimension=2, tiled=True)
    orbitals = shares[:, 0]
    response = shares[:, 1]
    density = lax.psum(jnp.sum(orbitals * response, axis=1), "occ") * occ_scale
    kernel = (weight[:, None] * (density[:, None] * orbitals + response)).astype(jnp.bfloat16)
    kernel_all = lax.all_gather(kernel, "occ", axis=1, tiled=True)
    partial_value = lax.dot_general(
        screened, kernel_all, (((0,), (0,)), ((), ())), preferred_element_type=jnp.float32
    )
    npoints = rows * grid_count
    return lax.psum_scatter(partial_value, "grid", scatter_dimension=1, tiled=True) / math.sqrt(
        npoints
    )


def solution(mesh):
    placed = (
        P("grid", "occ"),
        P("occ", "grid"),
        P("occ", "grid"),
        P("grid"),
        P("grid"),
        P("grid", "occ"),
    )
    return jax.shard_map(
        per_device, mesh=mesh, in_specs=placed, out_specs=P("occ", "grid"), check_vma=False
    )
```

profile of v0, /device:TPU:2, one launch (start us, length us, event | category | flops | bytes accessed | tf_op | source)
XLA Modules:
  0.0 392.5 jit_solution(2788873274233231226)
XLA Ops:
  6.5 0.0 copy-start
  6.5 0.0 all-gather.2.cloned.1.call-start
  6.5 1.5 pad_maximum_fusion
  8.0 0.0 all-gather.2.cloned.1.call-update
  8.0 0.0 reduce-scatter.3.cloned.1.call-start
  8.1 0.7 convert_element_type.8
  8.8 0.1 mul.39
  8.9 0.4 mul.40
  9.3 0.0 copy-done
  9.3 0.2 copy.8
  9.6 0.2 mul.41
  9.8 71.9 %all-gather.2.cloned.1.call-done = bf16[1000,1024]{0,1:T(8,128)(2,1)} async-done(((bf16[1000,32]{0,1:T(8,128)(2,1)}), bf16[1000,1024]{0,1:T(8,128)(2,1)}) %all-gather.2.cloned.1.call-update) | async-done | bytes 2048016 | tf_op jit(solution)/shard_map/all_gather | solution.py:28
  81.7 3.1 fusion.2
  84.8 0.0 copy-start.2
  84.8 0.0 copy-start.1
  84.8 1.6 copy.11
  86.4 0.0 reduce-scatter.3.cloned.1.call-update
  86.4 0.0 reduce-scatter.5.cloned.1.call-start
  86.5 0.0 copy-done.2
  86.5 0.1 iota_compare_fusion
  86.6 0.1 lt.14
  86.7 0.0 copy-done.1
  86.7 91.1 %reduce-scatter.3.cloned.1.call-done = f32[256,2,32]{0,2,1:T(8,128)} async-done(((f32[256,2,512]{0,2,1:T(8,128)}), f32[256,2,32]{0,2,1:T(8,128)}) %reduce-scatter.3.cloned.1.call-update) | async-done | bytes 65552 | tf_op jit(solution)/shard_map/reduce_scatter | solution.py:35
  177.7 0.8 multiply_reduce_fusion
  178.5 38.1 %psum.7 = f32[256]{0:T(256)S(1)} all-reduce(f32[256]{0:T(256)S(1)} %multiply_reduce_fusion), channel_id=1, replica_groups=mesh['grid'=32,'occ'=16] {'occ'}, use_global_device_ids=true, to_apply=%region_2.0 | all-reduce | flops 256 | bytes 2048 | tf_op jit(solution)/shard_map/psum | solution.py:38
  216.6 0.8 multiply_convert_fusion
  217.4 39.4 %all_gather.7 = bf16[256,512]{0,1:T(8,128)(2,1)S(1)} all-gather(bf16[256,32]{0,1:T(8,128)(2,1)S(1)} %multiply_convert_fusion), channel_id=1, replica_groups=mesh['grid'=32,'occ'=16] {'occ'}, dimensions={1}, use_global_device_ids=true | all-gather | bytes 278528 | tf_op jit(solution)/shard_map/all_gather | solution.py:40
  256.7 1.8 fusion.6
  258.5 0.0 reduce-scatter.5.cloned.1.call-update
  258.6 125.9 %reduce-scatter.5.cloned.1.call-done = f32[1000,16]{0,1:T(8,128)} async-done(((f32[1000,512]{0,1:T(8,128)}), f32[1000,16]{0,1:T(8,128)}) %reduce-scatter.5.cloned.1.call-update) | async-done | bytes 64016 | tf_op jit(solution)/shard_map/reduce_scatter | solution.py:45
  384.5 1.5 broadcast_multiply_fusion
  (2 shorter events, 0.0 us)
Async XLA Ops:
  6.5 2.8 copy-start
  6.5 75.2 %all-gather.2.cloned.1.call-start = ((), (), s32[]{:S(2)}) async-start(), calls=%async_computation.2 | async-start | bytes 2162688 | tf_op jit(solution)/shard_map/all_gather | solution.py:28
  8.0 169.7 %reduce-scatter.3.cloned.1.call-start = ((), (), s32[]{:S(2)}) async-start(), calls=%async_computation.3 | async-start | bytes 1114112 | tf_op jit(solution)/shard_map/reduce_scatter | solution.py:35
  84.8 1.7 copy-start.2
  84.8 1.9 copy-start.1
  86.4 298.0 %reduce-scatter.5.cloned.1.call-start = ((), (), s32[]{:S(2)}) async-start(), calls=%async_computation.4 | async-start | bytes 2162688 | tf_op jit(solution)/shard_map/reduce_scatter | solution.py:45
Sparse Core Ops, SparseCore 0:
  9.5 72.1 all-gather.1
  86.6 91.1 reduce-scatter.2
  258.7 125.7 reduce-scatter.4
where the time goes:
time: 393 us; the launch traced here: 392 us
  waiting for transfers between devices  289 us (74%)
  blocking collectives  77.4 us (20%)
  between operations  13.2 us (3%)
  other arithmetic  5.49 us (1%)
  matrix products  4.87 us (1%)
    reduce_scatter x1, waiting for transfers between devices, per_device(): lax.psum_scatter(partial_value, 'grid', scatter_dimension=1, tiled=True)  126 us
    reduce_scatter x1, waiting for transfers between devices, per_device(): shares = lax.psum_scatter(stacked, 'occ', scatter_dimension=2, tiled=True)  91.1 us
    all_gather x1, waiting for transfers between devices, per_device(): panels_all = lax.all_gather(joined, 'grid', axis=1, tiled=True)  71.9 us
    all_gather x1, blocking collectives, per_device(): kernel_all = lax.all_gather(kernel, 'occ', axis=1, tiled=True)  39.4 us
    psum x1, blocking collectives, per_device(): density = lax.psum(jnp.sum(orbitals * response, axis=1), 'occ') * occ_scale  38.1 us
  transfers between devices with their start and end apart: 3, of which 3 were waited for; matrix products, arithmetic and copies ran while one was open for 0% of the time, Pallas kernels for 0%

commit v1 on v0

--- a/solution.py
+++ b/solution.py
@@ -37,7 +37,9 @@
     response = shares[:, 1]
     density = lax.psum(jnp.sum(orbitals * response, axis=1), "occ") * occ_scale
     kernel = (weight[:, None] * (density[:, None] * orbitals + response)).astype(jnp.bfloat16)
-    kernel_all = lax.all_gather(kernel, "occ", axis=1, tiled=True)
+    kernel_all = jnp.concatenate(
+        lax.all_to_all(jnp.stack([kernel] * lax.axis_size("occ")), "occ", 0, 0), axis=1
+    )
     partial_value = lax.dot_general(
         screened, kernel_all, (((0,), (0,)), ((), ())), preferred_element_type=jnp.float32
     )

time: 393 us -> 367 us (0.934)
  blocking collectives: 77.4 us -> 56 us
  waiting for transfers between devices: 289 us -> 284 us
    all_gather x1 -> x0, blocking collectives: 39.4 us -> none  [per_device(): kernel_all = lax.all_gather(kernel, 'occ', axis=1, tiled=True)]
    all_to_all x0 -> x1, blocking collectives: none -> 17.9 us  [per_device(): lax.all_to_all(jnp.stack([kernel] * lax.axis_size('occ')), 'occ', 0, 0)]
    reduce_scatter x1, waiting for transfers between devices: 126 us -> 121 us  [per_device(): lax.psum_scatter(partial_value, 'grid', scatter_dimension=1, tiled=True)]
where the time goes in v1:
time: 367 us; the launch traced here: 366 us
  waiting for transfers between devices  284 us (77%)
  blocking collectives  56 us (15%)
  between operations  13.2 us (4%)
  other arithmetic  5.49 us (1%)
  matrix products  4.88 us (1%)
    reduce_scatter x1, waiting for transfers between devices, per_device(): lax.psum_scatter(partial_value, 'grid', scatter_dimension=1, tiled=True)  121 us
    reduce_scatter x1, waiting for transfers between devices, per_device(): shares = lax.psum_scatter(stacked, 'occ', scatter_dimension=2, tiled=True)  91.1 us
    all_gather x1, waiting for transfers between devices, per_device(): panels_all = lax.all_gather(joined, 'grid', axis=1, tiled=True)  71.9 us
    psum x1, blocking collectives, per_device(): density = lax.psum(jnp.sum(orbitals * response, axis=1), 'occ') * occ_scale  38.1 us
    all_to_all x1, blocking collectives, per_device(): lax.all_to_all(jnp.stack([kernel] * lax.axis_size('occ')), 'occ', 0, 0)  17.9 us
  transfers between devices with their start and end apart: 3, of which 3 were waited for; matrix products, arithmetic and copies ran while one was open for 0% of the time, Pallas kernels for 0%

profile of v1, /device:TPU:2, one launch (start us, length us, event | category | flops | bytes accessed | tf_op | source)
XLA Modules:
  0.0 366.1 jit_solution(7564510030865918474)
XLA Ops:
  6.5 0.0 copy-start
  6.5 0.0 all-gather.2.cloned.1.call-start
  6.5 1.5 pad_maximum_fusion
  8.0 0.0 all-gather.2.cloned.1.call-update
  8.0 0.0 reduce-scatter.3.cloned.1.call-start
  8.1 0.7 convert_element_type.10
  8.8 0.1 mul.43
  8.9 0.4 mul.44
  9.3 0.0 copy-done
  9.3 0.2 copy.8
  9.6 0.2 mul.45
  9.8 71.9 %all-gather.2.cloned.1.call-done = bf16[1000,1024]{0,1:T(8,128)(2,1)} async-done(((bf16[1000,32]{0,1:T(8,128)(2,1)}), bf16[1000,1024]{0,1:T(8,128)(2,1)}) %all-gather.2.cloned.1.call-update) | async-done | bytes 2048016 | tf_op jit(solution)/shard_map/all_gather | solution.py:28
  81.7 3.1 fusion.2
  84.8 0.0 copy-start.2
  84.8 0.0 copy-start.1
  84.8 1.6 copy.11
  86.4 0.0 reduce-scatter.3.cloned.1.call-update
  86.4 0.0 reduce-scatter.5.cloned.1.call-start
  86.5 0.0 copy-done.2
  86.5 0.1 iota_compare_fusion
  86.6 0.1 lt.14
  86.7 0.0 copy-done.1
  86.7 91.1 %reduce-scatter.3.cloned.1.call-done = f32[256,2,32]{0,2,1:T(8,128)} async-done(((f32[256,2,512]{0,2,1:T(8,128)}), f32[256,2,32]{0,2,1:T(8,128)}) %reduce-scatter.3.cloned.1.call-update) | async-done | bytes 65552 | tf_op jit(solution)/shard_map/reduce_scatter | solution.py:35
  177.7 0.8 multiply_reduce_fusion
  178.5 38.1 %psum.7 = f32[256]{0:T(256)S(1)} all-reduce(f32[256]{0:T(256)S(1)} %multiply_reduce_fusion), channel_id=1, replica_groups=mesh['grid'=32,'occ'=16] {'occ'}, use_global_device_ids=true, to_apply=%region_2.0 | all-reduce | flops 256 | bytes 2048 | tf_op jit(solution)/shard_map/psum | solution.py:38
  216.6 0.8 multiply_convert_fusion
  217.4 17.9 %all_to_all.5 = bf16[16,256,32]{1,2,0:T(8,128)(2,1)S(1)} all-to-all(bf16[16,256,32]{1,2,0:T(8,128)(2,1)S(1)} %stack.2), channel_id=1, replica_groups=mesh['grid'=32,'occ'=16] {'occ'}, dimensions={0} | all-to-all | bytes 524288 | tf_op jit(solution)/shard_map/all_to_all | solution.py:41
  235.3 1.8 fusion.6
  237.1 0.0 reduce-scatter.5.cloned.1.call-update
  237.2 120.9 %reduce-scatter.5.cloned.1.call-done = f32[1000,16]{0,1:T(8,128)} async-done(((f32[1000,512]{0,1:T(8,128)}), f32[1000,16]{0,1:T(8,128)}) %reduce-scatter.5.cloned.1.call-update) | async-done | bytes 64016 | tf_op jit(solution)/shard_map/reduce_scatter | solution.py:47
  358.1 1.5 broadcast_multiply_fusion
  (3 shorter events, 0.0 us)
Async XLA Ops:
  6.5 2.8 copy-start
  6.5 75.2 %all-gather.2.cloned.1.call-start = ((), (), s32[]{:S(2)}) async-start(), calls=%async_computation.3 | async-start | bytes 2162688 | tf_op jit(solution)/shard_map/all_gather | solution.py:28
  8.0 169.7 %reduce-scatter.3.cloned.1.call-start = ((), (), s32[]{:S(2)}) async-start(), calls=%async_computation.4 | async-start | bytes 1114112 | tf_op jit(solution)/shard_map/reduce_scatter | solution.py:35
  84.8 1.7 copy-start.2
  84.8 1.9 copy-start.1
  86.4 271.7 %reduce-scatter.5.cloned.1.call-start = ((), (), s32[]{:S(2)}) async-start(), calls=%async_computation.5 | async-start | bytes 2162688 | tf_op jit(solution)/shard_map/reduce_scatter | solution.py:47
Sparse Core Ops, SparseCore 0:
  9.5 72.1 all-gather.1
  86.6 91.1 reduce-scatter.2
  237.3 120.7 reduce-scatter.4
